TPU v7x, 32 devices: a whole 2x2x4 slice. The times are simulated.
32 devices in a mesh: band: 4 (over y, core), grid: 8 (over z, x).
Axes of the slice: x: 2, y: 2, z: 4, core: 2. Of those that a mesh axis runs over, the one named last changes fastest.
Arguments:
- wave: float32 [128, 64, 64, 128], P('grid', 'band'), may hold values from -1400 to 1400
- direction: float32 [128, 64, 64, 128], P('grid', 'band'), may hold values from -6 to 6
- potential: float32 [64, 64, 128], P('band', 'grid'), may hold values from -50 to 50
- rotation: float32 [384, 128], replicated, may hold values from -0.3125 to 0.3125
Outputs:
- new_block: float32 [128, 64, 64, 128], P(None, 'band', 'grid')
All inputs are finite; a program needn't handle non-finite values.
Results may differ from a plain program's by a relative error of at most 0.00016.
Values sent between devices are 32-bit elements; how exact they have to be, the bound alone decides.
No kernel may reach another device: no remote copies, remote signals or barrier semaphores. Data moves between devices by JAX's collectives and lax.ppermute only.
A program may use at most 704 MiB of HBM per device.

v0:
```python
import jax
import jax.numpy as jnp
from jax import lax
from jax.sharding import PartitionSpec as P

NX = 64
NY = 64
NZ = 128
STENCIL = (
    -5369.0 / 1800.0,
    12.0 / 7.0,
    -15.0 / 56.0,
    10.0 / 189.0,
    -1.0 / 112.0,
    2.0 / 1925.0,
    -1.0 / 16632.0,
)
LATTICE = 51.3


def with_halo(shard, sides, width):
    for axis, dim in sides:
        devices, length = (lax.axis_size(axis), shard.shape[dim])
        up = [(i, (i + 1) % devices) for i in range(devices)]
        down = [(j, i) for i, j in up]
        last = lax.slice_in_dim(shard, length - width, length, axis=dim)
        initial = lax.slice_in_dim(shard, 0, width, axis=dim)
        before = lax.ppermute(last, axis, up)
        after = lax.ppermute(initial, axis, down)
        shard = jnp.concatenate([before, shard, after], axis=dim)
    return shard


def axis_term(field, axis):
    total = STENCIL[0] * field
    for offset in range(1, 7):
        total = total + STENCIL[offset] * (
            jnp.roll(field, offset, axis) + jnp.roll(field, -offset, axis)
        )
    return total


def inner_products(stacked, ncells):
    high = lax.Precision.HIGHEST
    partial_sum = jnp.dot(stacked, stacked.T, precision=high) / ncells
    return lax.psum(partial_sum, ("band", "grid"))


def apply_basis(coefficients, stacked):
    return lax.dot_general(
        coefficients, stacked, (((0,), (0,)), ((), ())), precision=lax.Precision.HIGHEST
    )


def on_device(wave, direction, potential, rotation):
    local_pot = lax.all_gather(potential, "grid", axis=1, tiled=True)
    bands_here, planes, rows_y, depth = wave.shape
    total_x = planes * lax.axis_size("band")
    inverse_x = (total_x / LATTICE) ** 2
    inverse_y = (rows_y / LATTICE) ** 2
    inverse_z = (depth / LATTICE) ** 2
    padded = with_halo(wave, (("band", 1),), 6)
    along_x = STENCIL[0] * wave
    for offset in range(1, 7):
        along_x = along_x + STENCIL[offset] * (
            padded[:, 6 + offset : 6 + offset + planes]
            + padded[:, 6 - offset : 6 - offset + planes]
        )
    second = along_x * inverse_x + axis_term(wave, 2) * inverse_y + axis_term(wave, 3) * inverse_z
    hwave = -0.5 * second + local_pot[None] * wave
    ncells = NX * NY * NZ
    numer = jnp.sum(wave * hwave, axis=(1, 2, 3))
    denom = jnp.sum(wave * wave, axis=(1, 2, 3))
    numer, denom = lax.psum((numer, denom), "band")
    ritz = numer / denom
    resid = hwave - ritz[:, None, None, None] * wave
    rows_w, rows_r, rows_d = (
        lax.all_to_all(wave, "grid", split_axis=2, concat_axis=0, tiled=True),
        lax.all_to_all(resid, "grid", split_axis=2, concat_axis=0, tiled=True),
        lax.all_to_all(direction, "grid", split_axis=2, concat_axis=0, tiled=True),
    )
    total_bands = rows_w.shape[0]
    out_shape = rows_w.shape
    stacked = jnp.concatenate([rows_r, rows_w, rows_d], axis=0).reshape(3 * total_bands, -1)
    gram = inner_products(stacked, ncells)
    factor = jnp.linalg.cholesky(gram)
    solved = jax.scipy.linalg.solve_triangular(factor, rotation, lower=True, trans=1)
    mixed = apply_basis(solved, stacked)
    return mixed.reshape(out_shape)


def solution(mesh):
    return jax.shard_map(
        on_device,
        mesh=mesh,
        in_specs=(
            P("grid", "band", None, None),
            P("grid", "band", None, None),
            P("band", "grid", None),
            P(),
        ),
        out_specs=P(None, "band", "grid", None),
        check_vma=False,
    )
```

profile of v0, /device:TPU:0, one launch (start us, length us, event | category | flops | bytes accessed | tf_op | source)
XLA Modules:
  0.0 1144.8 jit_solution(8752095945358382932)
XLA Ops:
  6.5 14.2 %constant_dynamic-update-slice_fusion = (f32[16,22,64,128]{3,1,0,2:T(8,128)}, f32[16,16,64,128]{3,1,0,2:T(8,128)}) fusion(f32[16,16,64,128]{3,2,1,0:T(8,128)} %param.4), kind=kLoop, calls=%fused_computation.135 | loop fusion | bytes 25165824
  35.9 8.3 copy.155
  49.5 12.7 %fusion.103 = (f32[16,16,58,128]{3,1,0,2:T(8,128)}, f32[16,16,58,128]{3,1,0,2:T(8,128)}) fusion(f32[16,16,64,128]{3,1,0,2:T(8,128)} %get-tuple-element.30), kind=kLoop, calls=%fused_computation.159 | loop fusion | bytes 30408704 | tf_op jit(solution)/shard_map/jit(_roll_static)/slice | solution.py:38
  62.2 12.8 %fusion.101 = (f32[16,16,59,128]{3,1,0,2:T(8,128)}, f32[16,16,59,128]{3,1,0,2:T(8,128)}) fusion(f32[16,16,64,128]{3,1,0,2:T(8,128)} %get-tuple-element.30), kind=kLoop, calls=%fused_computation.157 | loop fusion | bytes 30932992 | tf_op jit(solution)/shard_map/jit(_roll_static)/slice | solution.py:38
  75.0 13.0 %fusion.99 = (f32[16,16,60,128]{3,1,0,2:T(8,128)}, f32[16,16,60,128]{3,1,0,2:T(8,128)}) fusion(f32[16,16,64,128]{3,1,0,2:T(8,128)} %get-tuple-element.30), kind=kLoop, calls=%fused_computation.155 | loop fusion | bytes 31457280 | tf_op jit(solution)/shard_map/jit(_roll_static)/slice | solution.py:38
  88.0 11.2 fusion.97
  99.2 11.6 %fusion.95 = (f32[16,16,62,128]{3,1,0,2:T(8,128)}, f32[16,16,62,128]{3,1,0,2:T(8,128)}) fusion(f32[16,16,64,128]{3,1,0,2:T(8,128)} %get-tuple-element.30), kind=kLoop, calls=%fused_computation.151 | loop fusion | bytes 32505856 | tf_op jit(solution)/shard_map/jit(_roll_static)/slice | solution.py:38
  183.5 27.6 %all-to-all-done.1 = f32[16,16,64,128]{3,1,0,2:T(8,128)} async-done(((f32[16,16,64,128]{3,1,0,2:T(8,128)}), f32[16,16,64,128]{3,1,0,2:T(8,128)}, u32[]{:S(2)}, u32[]{:S(2)}) %all-to-all-start.1) | async-done | bytes 8388640 | tf_op jit(solution)/shard_map/all_to_all | solution.py:78
  216.2 203.3 %all_gather.3 = f32[16,64,128]{2,1,0:T(8,128)S(1)} all-gather(f32[16,8,128]{2,1,0:T(8,128)S(1)} %copy-done.6), channel_id=1, replica_groups=mesh['band'=4,'grid'=8] {'grid'}, dimensions={1}, use_global_device_ids=true | all-gather | bytes 589824 | tf_op jit(solution)/shard_map/all_gather | solution.py:56
  425.7 13.0 %fusion.113 = (f32[16,16,64,123]{3,1,0,2:T(8,128)}, f32[16,16,64,123]{3,1,0,2:T(8,128)}) fusion(f32[16,16,64,128]{3,1,0,2:T(8,128)} %get-tuple-element.30), kind=kLoop, calls=%fused_computation.169 | loop fusion | bytes 32243712 | tf_op jit(solution)/shard_map/jit(_roll_static)/slice | solution.py:38
  465.4 149.9 %multiply_reduce_fusion.1 = (f32[16]{0:T(128)S(1)}, f32[16,16,64,128]{3,1,0,2:T(8,128)}) fusion(f32[16,16,64,128]{3,2,1,0:T(8,128)} %param.4, f32[16,16,64,128]{3,1,0,2:T(8,128)} %get-tuple-element.30, f32[16,64,128]{2,0,1:T(8,128)S(1)} %copy.146, f32[16,16,64,6]{3,1,0,2:T(8,128)} %get-tuple-element.76, f32[16,16,64,122]{3,1,0,2:T(8,128)} %get-tuple-element.78, ...), kind=kLoop, calls=%fused_computation.90 | loop fusion | flops 197132272 | bytes 280494144 | tf_op jit(solution)/shard_map/reduce_sum | solution.py:72
  621.0 14.0 %multiply_subtract_fusion = f32[16,16,64,128]{3,1,0,2:T(8,128)} fusion(f32[16,16,64,128]{3,1,0,2:T(8,128)} %get-tuple-element.24, f32[16]{0:T(128)S(1)} %div.17, f32[16,16,64,128]{3,2,1,0:T(8,128)} %param.4), kind=kLoop, calls=%fused_computation.88 | loop fusion | flops 4194304 | bytes 25165888 | tf_op jit(solution)/shard_map/sub | solution.py:76
  640.2 9.3 copy.154
  649.5 9.4 copy.157
  658.9 11.6 %copy.179 = f32[16,16,8,8,128]{4,3,1,0,2:T(8,128)} copy(f32[16,16,8,8,128]{4,1,0,3,2:T(8,128)} %bitcast.4) | data formatting | bytes 16777216 | tf_op jit(solution)/shard_map/all_to_all | solution.py:78
  670.5 9.6 concatenate.160
  680.0 11.6 %copy.178 = f32[16,16,8,8,128]{4,3,1,0,2:T(8,128)} copy(f32[16,16,8,8,128]{4,1,0,3,2:T(8,128)} %bitcast.8) | data formatting | bytes 16777216 | tf_op jit(solution)/shard_map/all_to_all | solution.py:80
  691.6 9.5 concatenate.161
  701.1 122.2 %all-to-all-done = f32[16,16,64,128]{3,1,0,2:T(8,128)} async-done(((f32[16,16,64,128]{3,1,0,2:T(8,128)}), f32[16,16,64,128]{3,1,0,2:T(8,128)}, u32[]{:S(2)}, u32[]{:S(2)}) %all-to-all-start) | async-done | bytes 8388640 | tf_op jit(solution)/shard_map/all_to_all | solution.py:79
  829.4 45.4 %fusion.61 = f32[384,384]{0,1:T(8,128)} fusion(f32[128,16,8,128]{3,0,2,1:T(8,128)} %bitcast.90, f32[128,16,8,128]{3,0,2,1:T(8,128)} %bitcast.89, f32[128,16,8,128]{3,0,2,1:T(8,128)S(1)} %bitcast.91), kind=kOutput, calls=%fused_computation.98 | convolution fusion | flops 29003759616 | bytes 25755648 | tf_op jit(solution)/shard_map/dot_general | solution.py:45
  874.8 11.6 %copy.180 = f32[16,16,8,8,128]{4,3,1,0,2:T(8,128)} copy(f32[16,16,8,8,128]{4,1,0,3,2:T(8,128)} %bitcast) | data formatting | bytes 16777216 | tf_op jit(solution)/shard_map/all_to_all | solution.py:79
  886.4 9.4 concatenate.159
  895.8 17.3 %maximum_bitcast_fusion = f32[16384,384]{0,1:T(8,128)} fusion(f32[128,16384]{1,0:T(8,128)} %concatenate.161, f32[128,16384]{1,0:T(8,128)} %concatenate.160, f32[128,16384]{1,0:T(8,128)} %concatenate.159), kind=kLoop, calls=%fused_computation.13 | loop fusion | flops 12582912 | bytes 50331648 | tf_op jit(solution)/shard_map/dot_general | solution.py:50
  913.1 24.9 %copy.160 = f32[16384,384]{1,0:T(8,128)} copy(f32[16384,384]{0,1:T(8,128)} %maximum_bitcast_fusion) | data formatting | bytes 50331648 | tf_op jit(solution)/shard_map/dot_general | solution.py:50
  938.0 63.3 %all-reduce.4.cloned.1.call-done = f32[384,384]{0,1:T(8,128)} async-done(((f32[384,384]{0,1:T(8,128)}), f32[384,384]{0,1:T(8,128)}) %all-reduce.4.cloned.1.call-update) | async-done | bytes 589840 | tf_op jit(solution)/shard_map/psum | solution.py:46
  1003.7 11.7 %cholesky.77 = f32[128,128]{1,0:T(8,128)S(1)} custom-call(f32[128,128]{1,0:T(8,128)S(1)} %cholesky.192), custom_call_target="Cholesky" | custom-call | tf_op jit(solution)/shard_map/jit(cholesky)/cholesky | solution.py:86
  1015.5 9.8 custom-call.23
  1025.9 11.7 %cholesky.162 = f32[128,128]{1,0:T(8,128)S(1)} custom-call(f32[128,128]{1,0:T(8,128)S(1)} %cholesky.196), custom_call_target="Cholesky" | custom-call | tf_op jit(solution)/shard_map/jit(cholesky)/cholesky | solution.py:86
  1037.6 10.0 custom-call.24
  1048.1 11.7 %cholesky.181 = f32[128,128]{1,0:T(8,128)S(1)} custom-call(f32[128,128]{1,0:T(8,128)S(1)} %convolution_subtract_fusion.3), custom_call_target="Cholesky" | custom-call | tf_op jit(solution)/shard_map/jit(cholesky)/cholesky | solution.py:86
  1068.9 29.5 %custom-call.25 = f32[3,128,128]{1,2,0:T(8,128)S(1)} custom-call(f32[3,128,128]{2,1,0:T(8,128)S(1)} %get-tuple-element.12), custom_call_target="InvertDiagBlocksLowerTriangular" | custom-call | tf_op jit(solution)/shard_map/jit(_solve_triangular)/triangular_solve | solution.py:87
  1099.7 29.5 %fusion.65 = f32[128,16,8,128]{3,0,2,1:T(8,128)S(1)} fusion(f32[16,8,128,384]{3,2,1,0:T(8,128)} %bitcast.85, f32[128,128]{1,0:T(8,128)S(1)} %fusion.77, f32[128,128]{1,0:T(8,128)S(1)} %fusion.79, f32[128,128]{1,0:T(8,128)S(1)} %fusion.80), kind=kOutput, calls=%fused_computation.104 | convolution fusion | flops 9663774720 | bytes 33751040 | tf_op jit(solution)/shard_map/dot_general | solution.py:50
  (99 shorter events, 173.9 us)
Async XLA Ops:
  20.7 190.4 %all-to-all-start.1 = ((f32[16,16,64,128]{3,1,0,2:T(8,128)}), f32[16,16,64,128]{3,1,0,2:T(8,128)}, u32[]{:S(2)}, u32[]{:S(2)}) async-start(f32[16,16,64,128]{3,1,0,2:T(8,128)} %get-tuple-element.30), calls=%async_computation.1 | async-start | bytes 16777216 | tf_op jit(solution)/shard_map/all_to_all | solution.py:78
  28.0 7.9 copy-start
  34.7 424.6 %collective-permute-start = (f32[16,6,64,128]{3,2,1,0:T(8,128)}, f32[16,6,64,128]{3,2,1,0:T(8,128)}, u32[]{:S(2)}, u32[]{:S(2)}) collective-permute-start(f32[16,6,64,128]{3,2,1,0:T(8,128)} %get-tuple-element.27), channel_id=1, source_target_pairs={{8,0},{16,8},{24,16},{0,24},{9,1},{17,9},{25,17},{1,25},{10,2},{18... | collective-permute-start | bytes 9437192 | tf_op jit(solution)/shard_map/ppermute | solution.py:29
  35.4 8.8 slice-start
  35.4 8.8 slice-start.1
  35.4 417.9 %collective-permute-start.1 = (f32[16,6,64,128]{3,2,1,0:T(8,128)}, f32[16,6,64,128]{3,2,1,0:T(8,128)}, u32[]{:S(2)}, u32[]{:S(2)}) collective-permute-start(f32[16,6,64,128]{3,2,1,0:T(8,128)} %get-tuple-element.28), channel_id=1, source_target_pairs={{0,8},{8,16},{16,24},{24,0},{1,9},{9,17},{17,25},{25,1},{2,10},{10... | collective-permute-start | bytes 9437192 | tf_op jit(solution)/shard_map/ppermute | solution.py:28
  88.0 22.8 %slice-start.2 = ((s8[8388608]{0:T(1024)(128)(4,1)}), s8[4194304]{0:T(1024)(128)(4,1)S(1)}, s32[]{:S(2)}) async-start(s8[8388608]{0:T(1024)(128)(4,1)} %bitcast.81), calls=%async_computation.6 | async-start | bytes 8388608
  99.2 11.6 %slice-start.3 = ((s8[8388608]{0:T(1024)(128)(4,1)}), s8[4194304]{0:T(1024)(128)(4,1)S(1)}, s32[]{:S(2)}) async-start(s8[8388608]{0:T(1024)(128)(4,1)} %bitcast.81), calls=%async_computation.7 | async-start | bytes 8388608
  183.5 32.7 %copy-start.6 = (f32[16,8,128]{2,1,0:T(8,128)S(1)}, f32[16,8,128]{2,1,0:T(8,128)}, u32[]{:S(2)}) copy-start(f32[16,8,128]{2,1,0:T(8,128)} %param.6) | copy-start | bytes 196612
  211.1 423.8 %all-to-all-start.2 = ((f32[16,16,64,128]{3,1,0,2:T(8,128)}), f32[16,16,64,128]{3,1,0,2:T(8,128)}, u32[]{:S(2)}, u32[]{:S(2)}) async-start(f32[16,16,64,128]{3,1,0,2:T(8,128)} %copy.155), calls=%async_computation.2 | async-start | bytes 16777216 | tf_op jit(solution)/shard_map/all_to_all | solution.py:80
  421.4 17.2 %slice-start.4 = ((s8[8388608]{0:T(1024)(128)(4,1)}), s8[4194304]{0:T(1024)(128)(4,1)S(1)}, s32[]{:S(2)}) async-start(s8[8388608]{0:T(1024)(128)(4,1)} %bitcast.83), calls=%async_computation.8 | async-start | bytes 8388608
  425.7 13.0 %slice-start.5 = ((s8[8388608]{0:T(1024)(128)(4,1)}), s8[4194304]{0:T(1024)(128)(4,1)S(1)}, s32[]{:S(2)}) async-start(s8[8388608]{0:T(1024)(128)(4,1)} %bitcast.83), calls=%async_computation.9 | async-start | bytes 8388608
  453.3 12.0 %copy-start.1 = (f32[16,16,6,128]{3,1,0,2:T(8,128)S(1)}, f32[16,16,6,128]{3,1,0,2:T(8,128)}, u32[]{:S(2)}) copy-start(f32[16,16,6,128]{3,1,0,2:T(8,128)} %get-tuple-element.51) | copy-start | bytes 2359300
  453.3 12.0 %copy-start.2 = (f32[16,16,6,128]{3,1,0,2:T(8,128)S(1)}, f32[16,16,6,128]{3,1,0,2:T(8,128)}, u32[]{:S(2)}) copy-start(f32[16,16,6,128]{3,1,0,2:T(8,128)} %get-tuple-element.52) | copy-start | bytes 2359300
  453.3 12.0 %copy-start.3 = (f32[16,16,5,128]{3,1,0,2:T(8,128)S(1)}, f32[16,16,5,128]{3,1,0,2:T(8,128)}, u32[]{:S(2)}) copy-start(f32[16,16,5,128]{3,1,0,2:T(8,128)} %get-tuple-element.47) | copy-start | bytes 1966084
  453.3 12.0 %copy-start.4 = (f32[16,16,5,128]{3,1,0,2:T(8,128)S(1)}, f32[16,16,5,128]{3,1,0,2:T(8,128)}, u32[]{:S(2)}) copy-start(f32[16,16,5,128]{3,1,0,2:T(8,128)} %get-tuple-element.48) | copy-start | bytes 1966084
  635.0 188.4 %all-to-all-start = ((f32[16,16,64,128]{3,1,0,2:T(8,128)}), f32[16,16,64,128]{3,1,0,2:T(8,128)}, u32[]{:S(2)}, u32[]{:S(2)}) async-start(f32[16,16,64,128]{3,1,0,2:T(8,128)} %multiply_subtract_fusion), calls=%async_computation | async-start | bytes 16777216 | tf_op jit(solution)/shard_map/all_to_all | solution.py:79
  640.0 361.3 %all-reduce.4.cloned.1.call-start = ((), (), s32[]{:S(2)}) async-start(), calls=%async_computation.3 | async-start | bytes 1179648 | tf_op jit(solution)/shard_map/psum | solution.py:46
  913.1 185.3 %copy-start.5 = (f32[384,128]{1,0:T(8,128)S(1)}, f32[384,128]{1,0:T(8,128)}, u32[]{:S(2)}) copy-start(f32[384,128]{1,0:T(8,128)} %param.7) | copy-start | bytes 589828
Sparse Core Ops, SparseCore 0:
  875.0 126.2 all-reduce.3
where the time goes:
time: 1150 us; the launch traced here: 1140 us
  local copies, waits for them, and re-layouts  338 us (29%)
  other arithmetic  273 us (24%)
  waiting for transfers between devices  213 us (19%)
  blocking collectives  209 us (18%)
  matrix products  77.2 us (7%)
  starting transfers between devices  18.7 us (2%)
  between operations  16 us (1%)
    all_gather x1, blocking collectives, on_device(): local_pot = lax.all_gather(potential, 'grid', axis=1, tiled=True)  203 us
    slice x24, local copies, waits for them, and re-layouts, axis_term(): jnp.roll(field, offset, axis) + jnp.roll(field, -offset, axis)  169 us
    reduce_sum x1, other arithmetic, on_device(): numer = jnp.sum(wave * hwave, axis=(1, 2, 3))  150 us
    all_to_all x1, waiting for transfers between devices, on_device(): lax.all_to_all(resid, 'grid', split_axis=2, concat_axis=0, tiled=True)  122 us
    psum x1, waiting for transfers between devices, inner_products(): return lax.psum(partial_sum, ('band', 'grid'))  63.3 us
    another operation x10, other arithmetic, on_device(): factor = jnp.linalg.cholesky(gram)  56.4 us
    dot_general x1, matrix products, inner_products(): partial_sum = jnp.dot(stacked, stacked.T, precision=high) / ncells  45.4 us
    dot_general x2, local copies, waits for them, and re-layouts, apply_basis(): lax.dot_general(coefficients, stacked, (((0,), (0,)), ((), ())), precisio...  33.1 us
  transfers between devices with their start and end apart: 6, of which 3 were waited for; matrix products, arithmetic and copies ran while one was open for 43% of the time, Pallas kernels for 0%

commit v1 on v0

--- a/solution.py
+++ b/solution.py
@@ -74,8 +74,33 @@
     numer, denom = lax.psum((numer, denom), "band")
     ritz = numer / denom
     resid = hwave - ritz[:, None, None, None] * wave
+
+    def run_the_flows(original):
+        mesh_name = "grid"
+        y2 = lax.axis_size(mesh_name)
+        block_last = lax.axis_index(mesh_name)
+        top, carry_out = (y2, block_last)
+        y_new = original.shape[2] // top
+        latest = jnp.roll(original, -carry_out * y_new, axis=2)
+        moved = lax.slice_in_dim(latest, 0, y_new, axis=2)
+        stack_in = [moved]
+        hop_no = 1
+        while hop_no < top:
+            m_next = lax.slice_in_dim(latest, hop_no * y_new, (hop_no + 1) * y_new, axis=2)
+            stack_in.append(
+                lax.ppermute(
+                    m_next,
+                    mesh_name,
+                    perm=[(dev_j, (dev_j + hop_no) % top) for dev_j in range(top)],
+                )
+            )
+            hop_no += 1
+        return jnp.roll(
+            jnp.concatenate(stack_in[::-1], axis=0), (carry_out + 1) * stack_in[0].shape[0], axis=0
+        )
+
     rows_w, rows_r, rows_d = (
-        lax.all_to_all(wave, "grid", split_axis=2, concat_axis=0, tiled=True),
+        run_the_flows(wave),
         lax.all_to_all(resid, "grid", split_axis=2, concat_axis=0, tiled=True),
         lax.all_to_all(direction, "grid", split_axis=2, concat_axis=0, tiled=True),
     )

time: 1150 us -> 1210 us (1.052)
  blocking collectives: 209 us -> 58.3 us
  starting transfers between devices: 18.7 us -> 140 us
  waiting for transfers between devices: 213 us -> 271 us
  local copies, waits for them, and re-layouts: 338 us -> 358 us
    ppermute x0 -> x7, waiting for transfers between devices: none -> 210 us  [run_the_flows(): lax.ppermute(m_next, mesh_name, perm=[(dev_j, (dev_j + hop_no) % top) for...]
    all_gather x1, blocking collectives: 203 us -> 52.6 us  [on_device(): local_pot = lax.all_gather(potential, 'grid', axis=1, tiled=True)]
    ppermute x0 -> x7, starting transfers between devices: none -> 125 us  [run_the_flows(): lax.ppermute(m_next, mesh_name, perm=[(dev_j, (dev_j + hop_no) % top) for...]
    all_to_all x1, waiting for transfers between devices: 122 us -> 0.01 us  [on_device(): lax.all_to_all(resid, 'grid', split_axis=2, concat_axis=0, tiled=True)]
    all_to_all x1 -> x0, waiting for transfers between devices: 27.6 us -> none  [on_device(): lax.all_to_all(wave, 'grid', split_axis=2, concat_axis=0, tiled=True)]
    unnamed x28 -> x30, local copies, waits for them, and re-layouts: 22.5 us -> 48.6 us
    all_to_all x2 -> x0, local copies, waits for them, and re-layouts: 20.9 us -> none  [on_device(): lax.all_to_all(wave, 'grid', split_axis=2, concat_axis=0, tiled=True)]
    dynamic_slice x0 -> x2, local copies, waits for them, and re-layouts: none -> 14 us  [run_the_flows(): jnp.roll(jnp.concatenate(stack_in[::-1], axis=0), (carry_out + 1) * stack...]
  transfers between devices with their start and end apart: 6 -> 12, of which waited for: 3 -> 4; matrix products, arithmetic and copies ran while one was open for 43% -> 43% of each run, Pallas kernels for 0% -> 0%
where the time goes in v1:
time: 1210 us; the launch traced here: 1200 us
  local copies, waits for them, and re-layouts  358 us (30%)
  other arithmetic  279 us (23%)
  waiting for transfers between devices  271 us (22%)
  starting transfers between devices  140 us (12%)
  matrix products  77 us (6%)
  blocking collectives  58.3 us (5%)
  between operations  16 us (1%)
    ppermute x7, waiting for transfers between devices, run_the_flows(): lax.ppermute(m_next, mesh_name, perm=[(dev_j, (dev_j + hop_no) % top) for...  210 us
    slice x24, local copies, waits for them, and re-layouts, axis_term(): jnp.roll(field, offset, axis) + jnp.roll(field, -offset, axis)  162 us
    reduce_sum x1, other arithmetic, on_device(): numer = jnp.sum(wave * hwave, axis=(1, 2, 3))  148 us
    ppermute x7, starting transfers between devices, run_the_flows(): lax.ppermute(m_next, mesh_name, perm=[(dev_j, (dev_j + hop_no) % top) for...  125 us
    psum x1, waiting for transfers between devices, inner_products(): return lax.psum(partial_sum, ('band', 'grid'))  61.3 us
    another operation x10, other arithmetic, on_device(): factor = jnp.linalg.cholesky(gram)  56.6 us
    all_gather x1, blocking collectives, on_device(): local_pot = lax.all_gather(potential, 'grid', axis=1, tiled=True)  52.6 us
    unnamed x30, local copies, waits for them, and re-layouts  48.6 us
  transfers between devices with their start and end apart: 12, of which 4 were waited for; matrix products, arithmetic and copies ran while one was open for 43% of the time, Pallas kernels for 0%

profile of v1, /device:TPU:0, one launch (start us, length us, event | category | flops | bytes accessed | tf_op | source)
XLA Modules:
  0.0 1200.0 jit_solution(4154248248084255472)
XLA Ops:
  30.0 14.1 %constant_dynamic-update-slice_fusion = (f32[16,22,64,128]{3,1,0,2:T(8,128)}, f32[16,16,64,128]{3,1,0,2:T(8,128)}) fusion(f32[16,16,64,128]{3,2,1,0:T(8,128)} %param.4), kind=kLoop, calls=%fused_computation.139 | loop fusion | bytes 25165824
  44.1 13.0 %fusion.105 = (f32[16,16,64,1]{3,1,0,2:T(8,128)}, f32[16,16,64,1]{3,1,0,2:T(8,128)}) fusion(f32[16,16,64,128]{3,1,0,2:T(8,128)} %get-tuple-element.30), kind=kLoop, calls=%fused_computation.179 | loop fusion | bytes 262144 | tf_op jit(solution)/shard_map/jit(_roll_static)/slice | solution.py:38
  134.2 13.1 %fusion.100 = (f32[16,16,60,128]{3,1,0,2:T(8,128)}, f32[16,16,60,128]{3,1,0,2:T(8,128)}) fusion(f32[16,16,64,128]{3,1,0,2:T(8,128)} %get-tuple-element.30), kind=kLoop, calls=%fused_computation.174 | loop fusion | bytes 31457280 | tf_op jit(solution)/shard_map/jit(_roll_static)/slice | solution.py:38
  147.4 12.9 %fusion.102 = (f32[16,16,59,128]{3,1,0,2:T(8,128)}, f32[16,16,59,128]{3,1,0,2:T(8,128)}) fusion(f32[16,16,64,128]{3,1,0,2:T(8,128)} %get-tuple-element.30), kind=kLoop, calls=%fused_computation.176 | loop fusion | bytes 30932992 | tf_op jit(solution)/shard_map/jit(_roll_static)/slice | solution.py:38
  160.3 12.7 %fusion.104 = (f32[16,16,58,128]{3,1,0,2:T(8,128)}, f32[16,16,58,128]{3,1,0,2:T(8,128)}) fusion(f32[16,16,64,128]{3,1,0,2:T(8,128)} %get-tuple-element.30), kind=kLoop, calls=%fused_computation.178 | loop fusion | bytes 30408704 | tf_op jit(solution)/shard_map/jit(_roll_static)/slice | solution.py:38
  182.5 52.6 %all_gather.3 = f32[16,64,128]{2,1,0:T(8,128)S(1)} all-gather(f32[16,8,128]{2,1,0:T(8,128)S(1)} %copy-done.3), channel_id=1, replica_groups=mesh['band'=4,'grid'=8] {'grid'}, dimensions={1}, use_global_device_ids=true | all-gather | bytes 589824 | tf_op jit(solution)/shard_map/all_gather | solution.py:56
  275.5 148.0 %multiply_reduce_fusion.1 = (f32[16]{0:T(128)S(1)}, f32[16,16,64,128]{3,1,0,2:T(8,128)}) fusion(f32[16,16,64,128]{3,2,1,0:T(8,128)} %param.4, f32[16,16,64,128]{3,1,0,2:T(8,128)} %get-tuple-element.30, f32[16,64,128]{2,0,1:T(8,128)S(1)} %copy.150, f32[16,16,64,6]{3,1,0,2:T(8,128)} %get-tuple-element.76, f32[16,16,64,122]{3,1,0,2:T(8,128)} %get-tuple-element.78, ...), kind=kLoop, calls=%fused_computation.92 | loop fusion | flops 197132272 | bytes 280494144 | tf_op jit(solution)/shard_map/reduce_sum | solution.py:72
  429.1 14.0 %multiply_subtract_fusion = f32[16,16,64,128]{3,1,0,2:T(8,128)} fusion(f32[16,16,64,128]{3,1,0,2:T(8,128)} %get-tuple-element.24, f32[16]{0:T(128)S(1)} %div.17, f32[16,16,64,128]{3,2,1,0:T(8,128)} %param.4), kind=kLoop, calls=%fused_computation.90 | loop fusion | flops 4194304 | bytes 25165888 | tf_op jit(solution)/shard_map/sub | solution.py:76
  449.7 13.3 %copy.156 = f32[16,16,64,128]{3,0,2,1:T(8,128)} copy(f32[16,16,64,128]{3,2,1,0:T(8,128)} %param.4) | data formatting | bytes 16777216 | tf_op args[0]
  463.0 8.4 fusion.6
  485.3 123.8 %collective-permute-done.2 = f32[16,16,8,128]{3,0,2,1:T(8,128)S(1)} collective-permute-done((f32[16,16,8,128]{3,0,2,1:T(8,128)S(1)}, f32[16,16,8,128]{3,0,2,1:T(8,128)S(1)}, u32[]{:S(2)}, u32[]{:S(2)}) %collective-permute-start.2) | collective-permute-done | bytes 1048608 | tf_op jit(solution)/shard_map/ppermute | solution.py:91
  609.2 22.5 %collective-permute-done.3 = f32[16,16,8,128]{3,0,2,1:T(8,128)S(1)} collective-permute-done((f32[16,16,8,128]{3,0,2,1:T(8,128)S(1)}, f32[16,16,8,128]{3,0,2,1:T(8,128)S(1)}, u32[]{:S(2)}, u32[]{:S(2)}) %collective-permute-start.3) | collective-permute-done | bytes 1048608 | tf_op jit(solution)/shard_map/ppermute | solution.py:91
  631.6 116.7 %collective-permute-start.8 = (f32[16,16,8,128]{3,0,2,1:T(8,128)}, f32[16,16,8,128]{3,0,2,1:T(8,128)}, u32[]{:S(2)}, u32[]{:S(2)}) collective-permute-start(f32[16,16,8,128]{3,0,2,1:T(8,128)} %get-tuple-element.79), channel_id=1, source_target_pairs={{0,1},{1,2},{2,3},{3,4},{4,5},{5,6},{6,7},{7,0},{8,9},{9,10},{10,1... | collective-permute-start | bytes 3145736 | tf_op jit(solution)/shard_map/ppermute | solution.py:91
  748.7 63.7 %collective-permute-done.5 = f32[16,16,8,128]{3,0,2,1:T(8,128)} collective-permute-done((f32[16,16,8,128]{3,0,2,1:T(8,128)}, f32[16,16,8,128]{3,0,2,1:T(8,128)}, u32[]{:S(2)}, u32[]{:S(2)}) %collective-permute-start.5) | collective-permute-done | bytes 1048608 | tf_op jit(solution)/shard_map/ppermute | solution.py:91
  830.8 9.6 copy.163
  840.4 9.0 copy.164
  849.4 9.3 copy.160
  858.7 11.6 copy.181
  870.3 9.4 concatenate.173
  885.8 45.3 %fusion.62 = f32[384,384]{0,1:T(8,128)} fusion(f32[128,16,8,128]{3,0,2,1:T(8,128)} %bitcast.77, f32[128,16,8,128]{3,0,2,1:T(8,128)} %constant_dynamic-slice_fusion.1, f32[128,16,8,128]{3,0,2,1:T(8,128)S(1)} %bitcast.78), kind=kOutput, calls=%fused_computation.102 | convolution fusion | flops 29003759616 | bytes 25755648 | tf_op jit(solution)/shard_map/dot_general | solution.py:45
  931.2 11.6 copy.182
  942.8 9.5 concatenate.171
  952.3 17.3 %maximum_bitcast_fusion = f32[16384,384]{0,1:T(8,128)} fusion(f32[128,16384]{1,0:T(8,128)} %concatenate.173, f32[128,16384]{1,0:T(8,128)} %copy.164, f32[128,16384]{1,0:T(8,128)} %concatenate.171), kind=kLoop, calls=%fused_computation.13 | loop fusion | flops 12582912 | bytes 50331648 | tf_op jit(solution)/shard_map/dot_general | solution.py:50
  969.6 25.0 %copy.165 = f32[16384,384]{1,0:T(8,128)} copy(f32[16384,384]{0,1:T(8,128)} %maximum_bitcast_fusion) | data formatting | bytes 50331648 | tf_op jit(solution)/shard_map/dot_general | solution.py:50
  994.6 61.3 %all-reduce.4.cloned.1.call-done = f32[384,384]{0,1:T(8,128)} async-done(((f32[384,384]{0,1:T(8,128)}), f32[384,384]{0,1:T(8,128)}) %all-reduce.4.cloned.1.call-update) | async-done | bytes 589840 | tf_op jit(solution)/shard_map/psum | solution.py:46
  1058.3 11.7 cholesky.77
  1070.1 9.8 custom-call.23
  1080.5 11.7 cholesky.162
  1092.3 10.2 custom-call.24
  1102.9 11.7 cholesky.181
  1124.5 29.5 %custom-call.25 = f32[3,128,128]{1,2,0:T(8,128)S(1)} custom-call(f32[3,128,128]{2,1,0:T(8,128)S(1)} %get-tuple-element.12), custom_call_target="InvertDiagBlocksLowerTriangular" | custom-call | tf_op jit(solution)/shard_map/jit(_solve_triangular)/triangular_solve | solution.py:112
  1155.3 29.4 %fusion.66 = f32[128,16,8,128]{3,0,2,1:T(8,128)S(1)} fusion(f32[16,8,128,384]{3,2,1,0:T(8,128)} %bitcast.73, f32[128,128]{1,0:T(8,128)S(1)} %fusion.78, f32[128,128]{1,0:T(8,128)S(1)} %fusion.80, f32[128,128]{1,0:T(8,128)S(1)} %fusion.81), kind=kOutput, calls=%fused_computation.108 | convolution fusion | flops 9663774720 | bytes 33751040 | tf_op jit(solution)/shard_map/dot_general | solution.py:50
  (114 shorter events, 228.4 us)
Async XLA Ops:
  6.5 9.2 copy-start.1
  13.3 256.2 %collective-permute-start = (f32[16,6,64,128]{3,2,1,0:T(8,128)}, f32[16,6,64,128]{3,2,1,0:T(8,128)}, u32[]{:S(2)}, u32[]{:S(2)}) collective-permute-start(f32[16,6,64,128]{3,2,1,0:T(8,128)} %get-tuple-element.27), channel_id=1, source_target_pairs={{8,0},{16,8},{24,16},{0,24},{9,1},{17,9},{25,17},{1,25},{10,2},{18... | collective-permute-start | bytes 9437192 | tf_op jit(solution)/shard_map/ppermute | solution.py:29
  15.7 248.0 %collective-permute-start.1 = (f32[16,6,64,128]{3,2,1,0:T(8,128)}, f32[16,6,64,128]{3,2,1,0:T(8,128)}, u32[]{:S(2)}, u32[]{:S(2)}) collective-permute-start(f32[16,6,64,128]{3,2,1,0:T(8,128)} %get-tuple-element.28), channel_id=1, source_target_pairs={{0,8},{8,16},{16,24},{24,0},{1,9},{9,17},{17,25},{25,1},{2,10},{10... | collective-permute-start | bytes 9437192 | tf_op jit(solution)/shard_map/ppermute | solution.py:28
  24.0 419.2 %all-to-all-start.1 = ((f32[16,16,64,128]{3,1,0,2:T(8,128)}), f32[16,16,64,128]{3,1,0,2:T(8,128)}, u32[]{:S(2)}, u32[]{:S(2)}) async-start(f32[16,16,64,128]{3,1,0,2:T(8,128)} %copy.158), calls=%async_computation.1 | async-start | bytes 16777216 | tf_op jit(solution)/shard_map/all_to_all | solution.py:105
  44.1 13.0 %copy-start = (f32[16,16,64,128]{3,1,0,2:T(8,128)S(1)}, f32[16,16,64,128]{3,1,0,2:T(8,128)}, u32[]{:S(2)}) copy-start(f32[16,16,64,128]{3,1,0,2:T(8,128)} %get-tuple-element.30) | copy-start | bytes 25165828
  173.0 9.5 copy-start.3
  174.6 66.8 %slice-start = ((s8[8388608]{0:T(1024)(128)(4,1)}), s8[4194304]{0:T(1024)(128)(4,1)S(1)}, s32[]{:S(2)}) async-start(s8[8388608]{0:T(1024)(128)(4,1)} %bitcast.71), calls=%async_computation.3 | async-start | bytes 8388608
  235.1 6.2 slice-start.1
  443.2 436.5 %all-to-all-start = ((f32[16,16,64,128]{3,1,0,2:T(8,128)}), f32[16,16,64,128]{3,1,0,2:T(8,128)}, u32[]{:S(2)}, u32[]{:S(2)}) async-start(f32[16,16,64,128]{3,1,0,2:T(8,128)} %multiply_subtract_fusion), calls=%async_computation | async-start | bytes 16777216 | tf_op jit(solution)/shard_map/all_to_all | solution.py:104
  449.4 606.4 %all-reduce.4.cloned.1.call-start = ((), (), s32[]{:S(2)}) async-start(), calls=%async_computation.2 | async-start | bytes 1179648 | tf_op jit(solution)/shard_map/psum | solution.py:46
  477.1 132.1 %collective-permute-start.2 = (f32[16,16,8,128]{3,0,2,1:T(8,128)S(1)}, f32[16,16,8,128]{3,0,2,1:T(8,128)S(1)}, u32[]{:S(2)}, u32[]{:S(2)}) collective-permute-start(f32[16,16,8,128]{3,0,2,1:T(8,128)S(1)} %get-tuple-element.85), channel_id=1, source_target_pairs={{0,7},{1,0},{2,1},{3,2},{4,3},{5,4},{6,5},{7,6},{8,15},{9,8},{10,9... | collective-permute-start | bytes 3145736 | tf_op jit(solution)/shard_map/ppermute | solution.py:91
  481.8 149.8 %collective-permute-start.3 = (f32[16,16,8,128]{3,0,2,1:T(8,128)S(1)}, f32[16,16,8,128]{3,0,2,1:T(8,128)S(1)}, u32[]{:S(2)}, u32[]{:S(2)}) collective-permute-start(f32[16,16,8,128]{3,0,2,1:T(8,128)S(1)} %get-tuple-element.84), channel_id=1, source_target_pairs={{0,6},{1,7},{2,0},{3,1},{4,2},{5,3},{6,4},{7,5},{8,14},{9,15},{10,... | collective-permute-start | bytes 3145736 | tf_op jit(solution)/shard_map/ppermute | solution.py:91
  482.4 266.2 %collective-permute-start.4 = (f32[16,16,8,128]{3,0,2,1:T(8,128)}, f32[16,16,8,128]{3,0,2,1:T(8,128)S(1)}, u32[]{:S(2)}, u32[]{:S(2)}) collective-permute-start(f32[16,16,8,128]{3,0,2,1:T(8,128)} %get-tuple-element.83), channel_id=1, source_target_pairs={{0,5},{1,6},{2,7},{3,0},{4,1},{5,2},{6,3},{7,4},{8,13},{9,14},{10,... | collective-permute-start | bytes 3145736 | tf_op jit(solution)/shard_map/ppermute | solution.py:91
  482.4 330.0 %collective-permute-start.5 = (f32[16,16,8,128]{3,0,2,1:T(8,128)}, f32[16,16,8,128]{3,0,2,1:T(8,128)}, u32[]{:S(2)}, u32[]{:S(2)}) collective-permute-start(f32[16,16,8,128]{3,0,2,1:T(8,128)} %get-tuple-element.82), channel_id=1, source_target_pairs={{0,4},{1,5},{2,6},{3,7},{4,0},{5,1},{6,2},{7,3},{8,12},{9,13},{10,... | collective-permute-start | bytes 3145736 | tf_op jit(solution)/shard_map/ppermute | solution.py:91
  485.3 328.5 %collective-permute-start.6 = (f32[16,16,8,128]{3,0,2,1:T(8,128)}, f32[16,16,8,128]{3,0,2,1:T(8,128)}, u32[]{:S(2)}, u32[]{:S(2)}) collective-permute-start(f32[16,16,8,128]{3,0,2,1:T(8,128)} %get-tuple-element.81), channel_id=1, source_target_pairs={{0,3},{1,4},{2,5},{3,6},{4,7},{5,0},{6,1},{7,2},{8,11},{9,12},{10,... | collective-permute-start | bytes 3145736 | tf_op jit(solution)/shard_map/ppermute | solution.py:91
  609.2 206.0 %collective-permute-start.7 = (f32[16,16,8,128]{3,0,2,1:T(8,128)}, f32[16,16,8,128]{3,0,2,1:T(8,128)}, u32[]{:S(2)}, u32[]{:S(2)}) collective-permute-start(f32[16,16,8,128]{3,0,2,1:T(8,128)} %get-tuple-element.80), channel_id=1, source_target_pairs={{0,2},{1,3},{2,4},{3,5},{4,6},{5,7},{6,0},{7,1},{8,10},{9,11},{10,... | collective-permute-start | bytes 3145736 | tf_op jit(solution)/shard_map/ppermute | solution.py:91
  631.6 184.9 %collective-permute-start.8 = (f32[16,16,8,128]{3,0,2,1:T(8,128)}, f32[16,16,8,128]{3,0,2,1:T(8,128)}, u32[]{:S(2)}, u32[]{:S(2)}) collective-permute-start(f32[16,16,8,128]{3,0,2,1:T(8,128)} %get-tuple-element.79), channel_id=1, source_target_pairs={{0,1},{1,2},{2,3},{3,4},{4,5},{5,6},{6,7},{7,0},{8,9},{9,10},{10,1... | collective-permute-start | bytes 3145736 | tf_op jit(solution)/shard_map/ppermute | solution.py:91
  969.6 184.4 %copy-start.2 = (f32[384,128]{1,0:T(8,128)S(1)}, f32[384,128]{1,0:T(8,128)}, u32[]{:S(2)}) copy-start(f32[384,128]{1,0:T(8,128)} %param.7) | copy-start | bytes 589828
Sparse Core Ops, SparseCore 0:
  931.3 124.5 all-reduce.3
